TPU v7x, 512 devices: a whole 4x4x16 slice. The times are simulated.
512 devices in a mesh: vec: 64 (over y, z), row: 8 (over x, core).
Axes of the slice: x: 4, y: 4, z: 16, core: 2. Of those that a mesh axis runs over, the one named last changes fastest.
Arguments:
- vectors: bfloat16 [8, 4096, 1024], P('row', 'vec'), may hold values from -6 to 6
- rotation: bfloat16 [1024, 1024], P(None, 'vec'), may hold values from -0.1875 to 0.1875
- blocks: bfloat16 [256, 8, 128, 128], P('row'), may hold values from -0.125 to 0.125
- column_blocks: int32 [256, 8], P('row'), may hold values from -2 to 257, as said below
Outputs:
- filtered: bfloat16 [8, 4096, 1024], P('row', 'vec')
Inputs may be any that keep to these rules, and one draw needn't show every extreme that they name: `column_blocks`: block row r of partition p = r // 32 lists 8 distinct column blocks between p * 32 - 2 and p * 32 + 33; the first block row of every partition lists the lowest of these and the last one the highest; column blocks outside 0 to 255 stand for zeros.
All inputs are finite; a program needn't handle non-finite values.
Results may differ from a plain program's by a relative error of at most 0.006.
Values may be sent and summed in bfloat16 or wider, within the bound.
A program may use at most 64 MiB of HBM per device.

v0:
```python
import jax
import jax.numpy as jnp
from jax import lax
from jax.sharding import PartitionSpec as P

BS = 128
HB = 2
STEPS = 4
centre = 0.3
half_width = 1.2


def with_halo(block, sides, width):
    for axis, dim in sides:
        count = lax.axis_size(axis)
        forward = [(i, i + 1) for i in range(count - 1)]
        backward = [(target, source) for source, target in forward]
        low = lax.ppermute(
            lax.slice_in_dim(block, block.shape[dim] - width, None, axis=dim), axis, forward
        )
        high = lax.ppermute(lax.slice_in_dim(block, 0, width, axis=dim), axis, backward)
        block = jnp.concatenate([low, block, high], axis=dim)
    return block


def apply_matrix(operand, blocks, offsets):
    extended = with_halo(operand, (("row", 1),), HB * BS)
    stacked = extended.reshape(extended.shape[0], -1, BS)
    picked = stacked[:, offsets]
    product = jnp.einsum("rjab,krjb->kra", blocks, picked, preferred_element_type=jnp.float32)
    return product.reshape(extended.shape[0], -1)


def filter_panel(vec_panel, blocks, offsets):
    previous = vec_panel.astype(jnp.float32)
    current = (apply_matrix(vec_panel, blocks, offsets) - centre * previous) / half_width
    for turn_index in range(STEPS - 1):
        operand = current.astype(jnp.bfloat16)
        following = (
            2.0 * (apply_matrix(operand, blocks, offsets) - centre * current) / half_width
            - previous
        )
        previous = current
        current = following
    return current.astype(jnp.bfloat16)


def local(vectors, rotation, blocks, column_blocks):
    local_rows = vectors[0]
    offsets = column_blocks - (lax.axis_index("row") * column_blocks.shape[0] - HB)
    contract = (((0,), (1,)), ((), ()))
    vec_panel = lax.dot_general(
        rotation,
        lax.all_gather(local_rows, "vec", axis=0, tiled=True),
        contract,
        preferred_element_type=jnp.float32,
    ).astype(jnp.bfloat16)
    filtered = filter_panel(vec_panel, blocks, offsets)
    returned = lax.all_to_all(filtered, "vec", split_axis=1, concat_axis=0, tiled=True)
    return jnp.transpose(returned)[None]


def solution(mesh):
    placed = (P("row", "vec", None), P(None, "vec"), P("row", None, None, None), P("row", None))
    return jax.shard_map(
        local, mesh=mesh, in_specs=placed, out_specs=P("row", "vec", None), check_vma=False
    )
```

profile of v0, /device:TPU:1, one launch (start us, length us, event | category | flops | bytes accessed | tf_op | source)
XLA Modules:
  0.0 266.6 jit_solution(13129486595092253713)
XLA Ops:
  6.5 0.7 all-gather.3.cloned.1.call-update
  7.3 0.7 compare_select_fusion
  8.1 156.6 %all-gather.3.cloned.1.call-done = bf16[1,4096,1024]{2,1,0:T(8,128)(2,1)} async-done(((bf16[1,64,1024]{2,1,0:T(8,128)(2,1)}), bf16[1,4096,1024]{2,1,0:T(8,128)(2,1)}) %all-gather.3.cloned.1.call-update) | async-done | bytes 8388624 | tf_op jit(solution)/shard_map/all_gather | solution.py:54
  164.7 5.7 %fusion.2 = bf16[16,4096]{1,0:T(8,128)(2,1)S(1)} fusion(bf16[1024,16]{0,1:T(8,128)(2,1)S(1)} %copy-done, bf16[1,4096,1024]{2,1,0:T(8,128)(2,1)} %all-gather.3.cloned.1.call-done), kind=kOutput, calls=%fused_computation.6 | convolution fusion | flops 134283264 | bytes 8552448 | tf_op jit(solution)/shard_map/dot_general | solution.py:52
  170.4 11.5 %collective-permute-start = (bf16[16,256]{1,0:T(8,128)(2,1)S(1)}, bf16[16,256]{1,0:T(8,128)(2,1)S(1)}, u32[]{:S(2)}, u32[]{:S(2)}) collective-permute-start(bf16[16,256]{1,0:T(8,128)(2,1)S(1)} %get-tuple-element.11), channel_id=1, source_target_pairs={{0,1},{1,2},{2,3},{3,4},{4,5},{5,6},{6,7},{8,9},{9,10},{10,11},{11... | collective-permute-start | bytes 24584 | tf_op jit(solution)/shard_map/ppermute | solution.py:18
  181.8 1.9 collective-permute-start.1
  183.8 3.0 %collective-permute-done.1 = bf16[16,256]{1,0:T(8,128)(2,1)S(1)} collective-permute-done((bf16[16,256]{1,0:T(8,128)(2,1)S(1)}, bf16[16,256]{1,0:T(8,128)(2,1)S(1)}, u32[]{:S(2)}, u32[]{:S(2)}) %collective-permute-start.1) | collective-permute-done | bytes 8224 | tf_op jit(solution)/shard_map/ppermute | solution.py:21
  186.8 0.8 gather_fusion
  187.7 5.7 %convolution_bitcast_fusion.3 = f32[32,2,8,128]{3,2,1,0:T(8,128)S(1)} fusion(bf16[16,32,8,128]{3,0,2,1:T(8,128)(2,1)S(1)} %bitcast.130, bf16[32,8,128,128]{3,2,1,0:T(8,128)(2,1)} %param.6), kind=kOutput, calls=%fused_computation.10 | convolution fusion | flops 134217728 | bytes 9699328 | tf_op jit(solution)/shard_map/rjab,krjb->kra/dot_general | solution.py:30
  193.4 1.9 collective-permute-start.2
  195.4 2.4 collective-permute-start.3
  197.8 2.6 collective-permute-done.3
  200.4 0.8 gather_fusion.1
  201.2 5.7 %convolution_bitcast_fusion.2 = f32[32,2,8,128]{3,2,1,0:T(8,128)S(1)} fusion(bf16[16,32,8,128]{3,0,2,1:T(8,128)(2,1)S(1)} %bitcast.131, bf16[32,8,128,128]{3,2,1,0:T(8,128)(2,1)} %param.6), kind=kOutput, calls=%fused_computation.9 | convolution fusion | flops 134217728 | bytes 9699328 | tf_op jit(solution)/shard_map/rjab,krjb->kra/dot_general | solution.py:30
  207.0 1.9 collective-permute-start.4
  209.0 2.4 collective-permute-start.5
  211.4 2.6 collective-permute-done.5
  214.0 0.8 gather_fusion.2
  214.8 5.7 %convolution_bitcast_fusion.1 = f32[32,2,8,128]{3,2,1,0:T(8,128)S(1)} fusion(bf16[16,32,8,128]{3,0,2,1:T(8,128)(2,1)S(1)} %bitcast.132, bf16[32,8,128,128]{3,2,1,0:T(8,128)(2,1)} %param.6), kind=kOutput, calls=%fused_computation.8 | convolution fusion | flops 134217728 | bytes 9699328 | tf_op jit(solution)/shard_map/rjab,krjb->kra/dot_general | solution.py:30
  220.5 0.1 fusion.12
  220.6 1.9 collective-permute-start.6
  222.6 2.4 collective-permute-start.7
  225.0 2.6 collective-permute-done.7
  227.6 0.8 gather_fusion.3
  228.4 5.7 %convolution_bitcast_fusion = f32[32,2,8,128]{3,2,1,0:T(8,128)S(1)} fusion(bf16[16,32,8,128]{3,0,2,1:T(8,128)(2,1)S(1)} %bitcast.129, bf16[32,8,128,128]{3,2,1,0:T(8,128)(2,1)} %param.6), kind=kOutput, calls=%fused_computation.7 | convolution fusion | flops 134217728 | bytes 9699328 | tf_op jit(solution)/shard_map/rjab,krjb->kra/dot_general | solution.py:30
  234.1 0.2 fusion.8
  234.3 0.2 all_to_all.14
  234.5 0.2 copy.72
  234.7 0.2 reshape.80
  234.9 23.9 %all_to_all.19 = bf16[64,2,512]{2,1,0:T(2,128)(2,1)S(1)} all-to-all(bf16[64,2,512]{2,1,0:T(2,128)(2,1)S(1)} %reshape.80), channel_id=1, replica_groups=mesh['vec'=64,'row'=8] {'vec'}, dimensions={0} | all-to-all | bytes 262144 | tf_op jit(solution)/shard_map/all_to_all | solution.py:59
  258.8 0.2 reshape.81
  259.0 0.8 copy.24
  (20 shorter events, 0.5 us)
Async XLA Ops:
  6.5 158.2 %copy-start = (bf16[1024,16]{0,1:T(8,128)(2,1)S(1)}, bf16[1024,16]{0,1:T(8,128)(2,1)}, u32[]{:S(2)}) copy-start(bf16[1024,16]{0,1:T(8,128)(2,1)} %param.5) | copy-start | bytes 98308
  6.5 158.2 %all-gather.3.cloned.1.call-start = ((), (), s32[]{:S(2)}) async-start(), calls=%async_computation.1 | async-start | bytes 8519680 | tf_op jit(solution)/shard_map/all_gather | solution.py:54
  170.4 13.4 %collective-permute-start = (bf16[16,256]{1,0:T(8,128)(2,1)S(1)}, bf16[16,256]{1,0:T(8,128)(2,1)S(1)}, u32[]{:S(2)}, u32[]{:S(2)}) collective-permute-start(bf16[16,256]{1,0:T(8,128)(2,1)S(1)} %get-tuple-element.11), channel_id=1, source_target_pairs={{0,1},{1,2},{2,3},{3,4},{4,5},{5,6},{6,7},{8,9},{9,10},{10,11},{11... | collective-permute-start | bytes 24584 | tf_op jit(solution)/shard_map/ppermute | solution.py:18
  181.8 5.0 %collective-permute-start.1 = (bf16[16,256]{1,0:T(8,128)(2,1)S(1)}, bf16[16,256]{1,0:T(8,128)(2,1)S(1)}, u32[]{:S(2)}, u32[]{:S(2)}) collective-permute-start(bf16[16,256]{1,0:T(8,128)(2,1)S(1)} %get-tuple-element.12), channel_id=1, source_target_pairs={{1,0},{2,1},{3,2},{4,3},{5,4},{6,5},{7,6},{9,8},{10,9},{11,10},{12... | collective-permute-start | bytes 24584 | tf_op jit(solution)/shard_map/ppermute | solution.py:21
  193.4 4.3 %collective-permute-start.2 = (bf16[16,256]{1,0:T(8,128)(2,1)S(1)}, bf16[16,256]{1,0:T(8,128)(2,1)S(1)}, u32[]{:S(2)}, u32[]{:S(2)}) collective-permute-start(bf16[16,256]{1,0:T(8,128)(2,1)S(1)} %get-tuple-element.9), channel_id=1, source_target_pairs={{0,1},{1,2},{2,3},{3,4},{4,5},{5,6},{6,7},{8,9},{9,10},{10,11},{11... | collective-permute-start | bytes 24584 | tf_op jit(solution)/shard_map/ppermute | solution.py:18
  195.4 5.0 %collective-permute-start.3 = (bf16[16,256]{1,0:T(8,128)(2,1)S(1)}, bf16[16,256]{1,0:T(8,128)(2,1)S(1)}, u32[]{:S(2)}, u32[]{:S(2)}) collective-permute-start(bf16[16,256]{1,0:T(8,128)(2,1)S(1)} %get-tuple-element.10), channel_id=1, source_target_pairs={{1,0},{2,1},{3,2},{4,3},{5,4},{6,5},{7,6},{9,8},{10,9},{11,10},{12... | collective-permute-start | bytes 24584 | tf_op jit(solution)/shard_map/ppermute | solution.py:21
  207.0 4.3 %collective-permute-start.4 = (bf16[16,256]{1,0:T(8,128)(2,1)S(1)}, bf16[16,256]{1,0:T(8,128)(2,1)S(1)}, u32[]{:S(2)}, u32[]{:S(2)}) collective-permute-start(bf16[16,256]{1,0:T(8,128)(2,1)S(1)} %get-tuple-element.7), channel_id=1, source_target_pairs={{0,1},{1,2},{2,3},{3,4},{4,5},{5,6},{6,7},{8,9},{9,10},{10,11},{11... | collective-permute-start | bytes 24584 | tf_op jit(solution)/shard_map/ppermute | solution.py:18
  209.0 5.0 %collective-permute-start.5 = (bf16[16,256]{1,0:T(8,128)(2,1)S(1)}, bf16[16,256]{1,0:T(8,128)(2,1)S(1)}, u32[]{:S(2)}, u32[]{:S(2)}) collective-permute-start(bf16[16,256]{1,0:T(8,128)(2,1)S(1)} %get-tuple-element.8), channel_id=1, source_target_pairs={{1,0},{2,1},{3,2},{4,3},{5,4},{6,5},{7,6},{9,8},{10,9},{11,10},{12... | collective-permute-start | bytes 24584 | tf_op jit(solution)/shard_map/ppermute | solution.py:21
  220.6 4.3 %collective-permute-start.6 = (bf16[16,256]{1,0:T(8,128)(2,1)S(1)}, bf16[16,256]{1,0:T(8,128)(2,1)S(1)}, u32[]{:S(2)}, u32[]{:S(2)}) collective-permute-start(bf16[16,256]{1,0:T(8,128)(2,1)S(1)} %get-tuple-element.5), channel_id=1, source_target_pairs={{0,1},{1,2},{2,3},{3,4},{4,5},{5,6},{6,7},{8,9},{9,10},{10,11},{11... | collective-permute-start | bytes 24584 | tf_op jit(solution)/shard_map/ppermute | solution.py:18
  222.6 5.0 %collective-permute-start.7 = (bf16[16,256]{1,0:T(8,128)(2,1)S(1)}, bf16[16,256]{1,0:T(8,128)(2,1)S(1)}, u32[]{:S(2)}, u32[]{:S(2)}) collective-permute-start(bf16[16,256]{1,0:T(8,128)(2,1)S(1)} %get-tuple-element.6), channel_id=1, source_target_pairs={{1,0},{2,1},{3,2},{4,3},{5,4},{6,5},{7,6},{9,8},{10,9},{11,10},{12... | collective-permute-start | bytes 24584 | tf_op jit(solution)/shard_map/ppermute | solution.py:21
Sparse Core Ops, SparseCore 0:
  10.3 154.3 all-gather.2
where the time goes:
time: 267 us
  waiting for transfers between devices  168 us (63%)
  matrix products  28.3 us (11%)
  starting transfers between devices  26.3 us (10%)
  blocking collectives  23.9 us (9%)
  between operations  13.6 us (5%)
  local copies, waits for them, and re-layouts  5.19 us (2%)
    all_gather x1, waiting for transfers between devices, local(): lax.all_gather(local_rows, 'vec', axis=0, tiled=True)  157 us
    all_to_all x1, blocking collectives, local(): lax.all_to_all(filtered, 'vec', split_axis=1, concat_axis=0, tiled=True)  23.9 us
    dot_general x4, matrix products, apply_matrix(): jnp.einsum('rjab,krjb->kra', blocks, picked, preferred_element_type=jnp.f...  22.6 us
    ppermute x4, starting transfers between devices, with_halo(): lax.ppermute(lax.slice_in_dim(block, block.shape[dim] - width, None, axis...  17.3 us
    ppermute x4, waiting for transfers between devices, with_halo(): lax.ppermute(lax.slice_in_dim(block, 0, width, axis=dim), axis, backward)  10.7 us
    ppermute x4, starting transfers between devices, with_halo(): lax.ppermute(lax.slice_in_dim(block, 0, width, axis=dim), axis, backward)  9.05 us
    dot_general x1, matrix products, local(): lax.dot_general(rotation, lax.all_gather(local_rows, 'vec', axis=0, tiled...  5.65 us
  transfers between devices with their start and end apart: 9, of which 5 were waited for; matrix products, arithmetic and copies ran while one was open for 0% of the time, Pallas kernels for 0%

commit v1 on v0

--- a/solution.py
+++ b/solution.py
@@ -8,6 +8,18 @@
 STEPS = 4
 centre = 0.3
 half_width = 1.2
+
+
+def collect(x, axis, dim):
+    ways, here = (lax.axis_size(axis), lax.axis_index(axis))
+    grown, reach = (x, 1)
+    while reach < ways:
+        theirs = lax.ppermute(grown, axis, [(d, d ^ reach) for d in range(ways)])
+        mine_first = jnp.concatenate([grown, theirs], axis=dim)
+        theirs_first = jnp.concatenate([theirs, grown], axis=dim)
+        grown = jnp.where(here & reach == 0, mine_first, theirs_first)
+        reach = 2 * reach
+    return grown
 
 
 def with_halo(block, sides, width):
@@ -50,10 +62,7 @@
     offsets = column_blocks - (lax.axis_index("row") * column_blocks.shape[0] - HB)
     contract = (((0,), (1,)), ((), ()))
     vec_panel = lax.dot_general(
-        rotation,
-        lax.all_gather(local_rows, "vec", axis=0, tiled=True),
-        contract,
-        preferred_element_type=jnp.float32,
+        rotation, collect(local_rows, "vec", 0), contract, preferred_element_type=jnp.float32
     ).astype(jnp.bfloat16)
     filtered = filter_panel(vec_panel, blocks, offsets)
     returned = lax.all_to_all(filtered, "vec", split_axis=1, concat_axis=0, tiled=True)

time: 267 us -> 425 us (1.59)
  waiting for transfers between devices: 168 us -> 240 us
  starting transfers between devices: 26.3 us -> 87.5 us
  blocking collectives: 23.9 us -> 52 us
  between operations: 13.6 us -> 0.38 us
  other arithmetic: 1.24 us -> 9.61 us
    ppermute x0 -> x6, waiting for transfers between devices: none -> 229 us  [collect(): theirs = lax.ppermute(grown, axis, [(d, d ^ reach) for d in range(ways)])]
    all_gather x1 -> x0, waiting for transfers between devices: 157 us -> none  [local(): lax.all_gather(local_rows, 'vec', axis=0, tiled=True)]
    ppermute x0 -> x6, starting transfers between devices: none -> 67.3 us  [collect(): theirs = lax.ppermute(grown, axis, [(d, d ^ reach) for d in range(ways)])]
    all_to_all x1, blocking collectives: 23.9 us -> 52 us  [local(): lax.all_to_all(filtered, 'vec', split_axis=1, concat_axis=0, tiled=True)]
    select_n x0 -> x5, other arithmetic: none -> 9.06 us  [collect(): grown = jnp.where(here & reach == 0, mine_first, theirs_first)]
    ppermute x4, starting transfers between devices: 17.3 us -> 11.1 us  [with_halo(): lax.ppermute(lax.slice_in_dim(block, block.shape[dim] - width, None, axis...]
  transfers between devices with their start and end apart: 9 -> 14, of which waited for: 5 -> 10; matrix products, arithmetic and copies ran while one was open for 0% -> 0% of each run, Pallas kernels for 0% -> 0%
where the time goes in v1:
time: 425 us; the launch traced here: 424 us
  waiting for transfers between devices  240 us (56%)
  starting transfers between devices  87.5 us (21%)
  blocking collectives  52 us (12%)
  matrix products  29.7 us (7%)
  other arithmetic  9.61 us (2%)
  local copies, waits for them, and re-layouts  5.19 us (1%)
    ppermute x6, waiting for transfers between devices, collect(): theirs = lax.ppermute(grown, axis, [(d, d ^ reach) for d in range(ways)])  229 us
    ppermute x6, starting transfers between devices, collect(): theirs = lax.ppermute(grown, axis, [(d, d ^ reach) for d in range(ways)])  67.3 us
    all_to_all x1, blocking collectives, local(): lax.all_to_all(filtered, 'vec', split_axis=1, concat_axis=0, tiled=True)  52 us
    dot_general x4, matrix products, apply_matrix(): jnp.einsum('rjab,krjb->kra', blocks, picked, preferred_element_type=jnp.f...  22.6 us
    ppermute x4, starting transfers between devices, with_halo(): lax.ppermute(lax.slice_in_dim(block, block.shape[dim] - width, None, axis...  11.1 us
    ppermute x4, waiting for transfers between devices, with_halo(): lax.ppermute(lax.slice_in_dim(block, 0, width, axis=dim), axis, backward)  10.7 us
    select_n x5, other arithmetic, collect(): grown = jnp.where(here & reach == 0, mine_first, theirs_first)  9.06 us
    ppermute x4, starting transfers between devices, with_halo(): lax.ppermute(lax.slice_in_dim(block, 0, width, axis=dim), axis, backward)  9.05 us
  transfers between devices with their start and end apart: 14, of which 10 were waited for; matrix products, arithmetic and copies ran while one was open for 0% of the time, Pallas kernels for 0%

profile of v1, /device:TPU:1, one launch (start us, length us, event | category | flops | bytes accessed | tf_op | source)
XLA Modules:
  0.0 423.9 jit_solution(4378814530193492054)
XLA Ops:
  0.0 4.5 %collective-permute-start = (bf16[64,1024]{1,0:T(8,128)(2,1)}, bf16[64,1024]{1,0:T(8,128)(2,1)S(1)}, u32[]{:S(2)}, u32[]{:S(2)}) collective-permute-start(bf16[64,1024]{1,0:T(8,128)(2,1)} %bitcast.133), channel_id=1, source_target_pairs={{0,8},{8,0},{16,24},{24,16},{32,40},{40,32},{48,56},{56,48},{64,72... | collective-permute-start | bytes 393224 | tf_op jit(solution)/shard_map/ppermute | solution.py:17
  4.5 2.5 collective-permute-done
  8.1 5.7 %collective-permute-start.1 = (bf16[128,1024]{1,0:T(8,128)(2,1)S(1)}, bf16[128,1024]{1,0:T(8,128)(2,1)S(1)}, u32[]{:S(2)}, u32[]{:S(2)}) collective-permute-start(bf16[128,1024]{1,0:T(8,128)(2,1)S(1)} %maximum_select_fusion.10), channel_id=1, source_target_pairs={{0,16},{8,24},{16,0},{24,8},{32,48},{40,56},{48,32},{56,40},{64,80... | collective-permute-start | bytes 786440 | tf_op jit(solution)/shard_map/ppermute | solution.py:17
  13.8 6.6 %collective-permute-done.1 = bf16[128,1024]{1,0:T(8,128)(2,1)S(1)} collective-permute-done((bf16[128,1024]{1,0:T(8,128)(2,1)S(1)}, bf16[128,1024]{1,0:T(8,128)(2,1)S(1)}, u32[]{:S(2)}, u32[]{:S(2)}) %collective-permute-start.1) | collective-permute-done | bytes 262176 | tf_op jit(solution)/shard_map/ppermute | solution.py:17
  20.5 13.6 %collective-permute-start.2 = (bf16[256,1024]{1,0:T(8,128)(2,1)S(1)}, bf16[256,1024]{1,0:T(8,128)(2,1)S(1)}, u32[]{:S(2)}, u32[]{:S(2)}) collective-permute-start(bf16[256,1024]{1,0:T(8,128)(2,1)S(1)} %maximum_select_fusion.9), channel_id=1, source_target_pairs={{0,32},{8,40},{16,48},{24,56},{32,0},{40,8},{48,16},{56,24},{64,96... | collective-permute-start | bytes 1572872 | tf_op jit(solution)/shard_map/ppermute | solution.py:17
  34.1 45.1 %collective-permute-done.2 = bf16[256,1024]{1,0:T(8,128)(2,1)S(1)} collective-permute-done((bf16[256,1024]{1,0:T(8,128)(2,1)S(1)}, bf16[256,1024]{1,0:T(8,128)(2,1)S(1)}, u32[]{:S(2)}, u32[]{:S(2)}) %collective-permute-start.2) | collective-permute-done | bytes 524320 | tf_op jit(solution)/shard_map/ppermute | solution.py:17
  79.6 35.6 %collective-permute-start.3 = (bf16[512,1024]{1,0:T(8,128)(2,1)S(1)}, bf16[512,1024]{1,0:T(8,128)(2,1)}, u32[]{:S(2)}, u32[]{:S(2)}) collective-permute-start(bf16[512,1024]{1,0:T(8,128)(2,1)S(1)} %maximum_select_fusion.8), channel_id=1, source_target_pairs={{0,64},{8,72},{16,80},{24,88},{32,96},{40,104},{48,112},{56,120},{... | collective-permute-start | bytes 3145736 | tf_op jit(solution)/shard_map/ppermute | solution.py:17
  115.2 39.8 %collective-permute-done.3 = bf16[512,1024]{1,0:T(8,128)(2,1)} collective-permute-done((bf16[512,1024]{1,0:T(8,128)(2,1)S(1)}, bf16[512,1024]{1,0:T(8,128)(2,1)}, u32[]{:S(2)}, u32[]{:S(2)}) %collective-permute-start.3) | collective-permute-done | bytes 1048608 | tf_op jit(solution)/shard_map/ppermute | solution.py:17
  155.0 2.5 maximum_select_fusion.7
  157.5 3.2 collective-permute-start.4
  160.7 45.5 %collective-permute-done.4 = bf16[1024,1024]{1,0:T(8,128)(2,1)} collective-permute-done((bf16[1024,1024]{1,0:T(8,128)(2,1)S(1)}, bf16[1024,1024]{1,0:T(8,128)(2,1)}, u32[]{:S(2)}, u32[]{:S(2)}) %collective-permute-start.4) | collective-permute-done | bytes 2097184 | tf_op jit(solution)/shard_map/ppermute | solution.py:17
  206.2 4.9 %maximum_select_fusion.6 = bf16[2048,1024]{1,0:T(8,128)(2,1)} fusion(bf16[1024,1024]{1,0:T(8,128)(2,1)} %collective-permute-done.4, bf16[1024,1024]{1,0:T(8,128)(2,1)S(1)} %maximum_select_fusion.7, pred[]{:T(512)S(6)} %eq.19), kind=kLoop, calls=%fused_computation.14 | loop fusion | flops 18874368 | bytes 8388609 | tf_op jit(solution)/shard_map/jit(_where)/select_n | solution.py:20
  211.1 4.8 %collective-permute-start.5 = (bf16[2048,1024]{1,0:T(8,128)(2,1)}, bf16[2048,1024]{1,0:T(8,128)(2,1)}, u32[]{:S(2)}, u32[]{:S(2)}) collective-permute-start(bf16[2048,1024]{1,0:T(8,128)(2,1)} %maximum_select_fusion.6), channel_id=1, source_target_pairs={{0,256},{8,264},{16,272},{24,280},{32,288},{40,296},{48,304},{56,3... | collective-permute-start | bytes 12582920 | tf_op jit(solution)/shard_map/ppermute | solution.py:17
  216.1 89.4 %collective-permute-done.5 = bf16[2048,1024]{1,0:T(8,128)(2,1)} collective-permute-done((bf16[2048,1024]{1,0:T(8,128)(2,1)}, bf16[2048,1024]{1,0:T(8,128)(2,1)}, u32[]{:S(2)}, u32[]{:S(2)}) %collective-permute-start.5) | collective-permute-done | bytes 4194336 | tf_op jit(solution)/shard_map/ppermute | solution.py:17
  305.5 7.1 %fusion.8 = bf16[16,4096]{1,0:T(8,128)(2,1)S(1)} fusion(bf16[1024,16]{0,1:T(8,128)(2,1)S(1)} %copy-done, bf16[2048,1024]{1,0:T(8,128)(2,1)} %collective-permute-done.5, bf16[2048,1024]{1,0:T(8,128)(2,1)} %maximum_select_fusion.6, pred[]{:T(512)S(6)} %eq.18), kind=kOutput, calls=%fused_computation.13 | convolution fusion | flops 172032000 | bytes 8552449 | tf_op jit(solution)/shard_map/dot_general | solution.py:64
  312.6 5.3 %collective-permute-start.6 = (bf16[16,256]{1,0:T(8,128)(2,1)S(1)}, bf16[16,256]{1,0:T(8,128)(2,1)S(1)}, u32[]{:S(2)}, u32[]{:S(2)}) collective-permute-start(bf16[16,256]{1,0:T(8,128)(2,1)S(1)} %get-tuple-element.11), channel_id=1, source_target_pairs={{0,1},{1,2},{2,3},{3,4},{4,5},{5,6},{6,7},{8,9},{9,10},{10,11},{11... | collective-permute-start | bytes 24584 | tf_op jit(solution)/shard_map/ppermute | solution.py:30
  317.9 1.9 collective-permute-start.7
  319.8 3.0 collective-permute-done.7
  323.7 5.7 %convolution_bitcast_fusion.3 = f32[32,2,8,128]{3,2,1,0:T(8,128)S(1)} fusion(bf16[16,32,8,128]{3,0,2,1:T(8,128)(2,1)S(1)} %bitcast.128, bf16[32,8,128,128]{3,2,1,0:T(8,128)(2,1)} %param.6), kind=kOutput, calls=%fused_computation.19 | convolution fusion | flops 134217728 | bytes 9699328 | tf_op jit(solution)/shard_map/rjab,krjb->kra/dot_general | solution.py:42
  329.5 1.9 collective-permute-start.8
  331.4 2.4 collective-permute-start.9
  333.8 2.6 collective-permute-done.9
  337.3 5.7 %convolution_bitcast_fusion.2 = f32[32,2,8,128]{3,2,1,0:T(8,128)S(1)} fusion(bf16[16,32,8,128]{3,0,2,1:T(8,128)(2,1)S(1)} %bitcast.129, bf16[32,8,128,128]{3,2,1,0:T(8,128)(2,1)} %param.6), kind=kOutput, calls=%fused_computation.18 | convolution fusion | flops 134217728 | bytes 9699328 | tf_op jit(solution)/shard_map/rjab,krjb->kra/dot_general | solution.py:42
  343.0 1.9 collective-permute-start.10
  345.0 2.4 collective-permute-start.11
  347.4 2.6 collective-permute-done.11
  350.8 5.7 %convolution_bitcast_fusion.1 = f32[32,2,8,128]{3,2,1,0:T(8,128)S(1)} fusion(bf16[16,32,8,128]{3,0,2,1:T(8,128)(2,1)S(1)} %bitcast.130, bf16[32,8,128,128]{3,2,1,0:T(8,128)(2,1)} %param.6), kind=kOutput, calls=%fused_computation.17 | convolution fusion | flops 134217728 | bytes 9699328 | tf_op jit(solution)/shard_map/rjab,krjb->kra/dot_general | solution.py:42
  356.6 1.9 collective-permute-start.12
  358.6 2.4 collective-permute-start.13
  361.0 2.6 collective-permute-done.13
  364.4 5.7 %convolution_bitcast_fusion = f32[32,2,8,128]{3,2,1,0:T(8,128)S(1)} fusion(bf16[16,32,8,128]{3,0,2,1:T(8,128)(2,1)S(1)} %bitcast.127, bf16[32,8,128,128]{3,2,1,0:T(8,128)(2,1)} %param.6), kind=kOutput, calls=%fused_computation.16 | convolution fusion | flops 134217728 | bytes 9699328 | tf_op jit(solution)/shard_map/rjab,krjb->kra/dot_general | solution.py:42
  370.9 52.0 %all_to_all.19 = bf16[64,2,512]{2,1,0:T(2,128)(2,1)S(1)} all-to-all(bf16[64,2,512]{2,1,0:T(2,128)(2,1)S(1)} %reshape.79), channel_id=1, replica_groups=mesh['vec'=64,'row'=8] {'vec'}, dimensions={0} | all-to-all | bytes 262144 | tf_op jit(solution)/shard_map/all_to_all | solution.py:68
  (36 shorter events, 7.4 us)
Async XLA Ops:
  0.0 305.5 %copy-start = (bf16[1024,16]{0,1:T(8,128)(2,1)S(1)}, bf16[1024,16]{0,1:T(8,128)(2,1)}, u32[]{:S(2)}) copy-start(bf16[1024,16]{0,1:T(8,128)(2,1)} %param.5) | copy-start | bytes 98308
  0.0 7.1 %collective-permute-start = (bf16[64,1024]{1,0:T(8,128)(2,1)}, bf16[64,1024]{1,0:T(8,128)(2,1)S(1)}, u32[]{:S(2)}, u32[]{:S(2)}) collective-permute-start(bf16[64,1024]{1,0:T(8,128)(2,1)} %bitcast.133), channel_id=1, source_target_pairs={{0,8},{8,0},{16,24},{24,16},{32,40},{40,32},{48,56},{56,48},{64,72... | collective-permute-start | bytes 393224 | tf_op jit(solution)/shard_map/ppermute | solution.py:17
  8.1 12.2 %collective-permute-start.1 = (bf16[128,1024]{1,0:T(8,128)(2,1)S(1)}, bf16[128,1024]{1,0:T(8,128)(2,1)S(1)}, u32[]{:S(2)}, u32[]{:S(2)}) collective-permute-start(bf16[128,1024]{1,0:T(8,128)(2,1)S(1)} %maximum_select_fusion.10), channel_id=1, source_target_pairs={{0,16},{8,24},{16,0},{24,8},{32,48},{40,56},{48,32},{56,40},{64,80... | collective-permute-start | bytes 786440 | tf_op jit(solution)/shard_map/ppermute | solution.py:17
  20.5 58.7 %collective-permute-start.2 = (bf16[256,1024]{1,0:T(8,128)(2,1)S(1)}, bf16[256,1024]{1,0:T(8,128)(2,1)S(1)}, u32[]{:S(2)}, u32[]{:S(2)}) collective-permute-start(bf16[256,1024]{1,0:T(8,128)(2,1)S(1)} %maximum_select_fusion.9), channel_id=1, source_target_pairs={{0,32},{8,40},{16,48},{24,56},{32,0},{40,8},{48,16},{56,24},{64,96... | collective-permute-start | bytes 1572872 | tf_op jit(solution)/shard_map/ppermute | solution.py:17
  79.6 75.3 %collective-permute-start.3 = (bf16[512,1024]{1,0:T(8,128)(2,1)S(1)}, bf16[512,1024]{1,0:T(8,128)(2,1)}, u32[]{:S(2)}, u32[]{:S(2)}) collective-permute-start(bf16[512,1024]{1,0:T(8,128)(2,1)S(1)} %maximum_select_fusion.8), channel_id=1, source_target_pairs={{0,64},{8,72},{16,80},{24,88},{32,96},{40,104},{48,112},{56,120},{... | collective-permute-start | bytes 3145736 | tf_op jit(solution)/shard_map/ppermute | solution.py:17
  157.5 48.7 %collective-permute-start.4 = (bf16[1024,1024]{1,0:T(8,128)(2,1)S(1)}, bf16[1024,1024]{1,0:T(8,128)(2,1)}, u32[]{:S(2)}, u32[]{:S(2)}) collective-permute-start(bf16[1024,1024]{1,0:T(8,128)(2,1)S(1)} %maximum_select_fusion.7), channel_id=1, source_target_pairs={{0,128},{8,136},{16,144},{24,152},{32,160},{40,168},{48,176},{56,1... | collective-permute-start | bytes 6291464 | tf_op jit(solution)/shard_map/ppermute | solution.py:17
  160.7 55.2 %copy-start.1 = (s32[32,8]{0,1:T(8,128)S(1)}, s32[32,8]{0,1:T(8,128)}, u32[]{:S(2)}) copy-start(s32[32,8]{0,1:T(8,128)} %param.7) | copy-start | bytes 3076
  211.1 94.4 %collective-permute-start.5 = (bf16[2048,1024]{1,0:T(8,128)(2,1)}, bf16[2048,1024]{1,0:T(8,128)(2,1)}, u32[]{:S(2)}, u32[]{:S(2)}) collective-permute-start(bf16[2048,1024]{1,0:T(8,128)(2,1)} %maximum_select_fusion.6), channel_id=1, source_target_pairs={{0,256},{8,264},{16,272},{24,280},{32,288},{40,296},{48,304},{56,3... | collective-permute-start | bytes 12582920 | tf_op jit(solution)/shard_map/ppermute | solution.py:17
  312.6 7.2 %collective-permute-start.6 = (bf16[16,256]{1,0:T(8,128)(2,1)S(1)}, bf16[16,256]{1,0:T(8,128)(2,1)S(1)}, u32[]{:S(2)}, u32[]{:S(2)}) collective-permute-start(bf16[16,256]{1,0:T(8,128)(2,1)S(1)} %get-tuple-element.11), channel_id=1, source_target_pairs={{0,1},{1,2},{2,3},{3,4},{4,5},{5,6},{6,7},{8,9},{9,10},{10,11},{11... | collective-permute-start | bytes 24584 | tf_op jit(solution)/shard_map/ppermute | solution.py:30
  317.9 5.0 %collective-permute-start.7 = (bf16[16,256]{1,0:T(8,128)(2,1)S(1)}, bf16[16,256]{1,0:T(8,128)(2,1)S(1)}, u32[]{:S(2)}, u32[]{:S(2)}) collective-permute-start(bf16[16,256]{1,0:T(8,128)(2,1)S(1)} %get-tuple-element.12), channel_id=1, source_target_pairs={{1,0},{2,1},{3,2},{4,3},{5,4},{6,5},{7,6},{9,8},{10,9},{11,10},{12... | collective-permute-start | bytes 24584 | tf_op jit(solution)/shard_map/ppermute | solution.py:33
  329.5 4.3 %collective-permute-start.8 = (bf16[16,256]{1,0:T(8,128)(2,1)S(1)}, bf16[16,256]{1,0:T(8,128)(2,1)S(1)}, u32[]{:S(2)}, u32[]{:S(2)}) collective-permute-start(bf16[16,256]{1,0:T(8,128)(2,1)S(1)} %get-tuple-element.9), channel_id=1, source_target_pairs={{0,1},{1,2},{2,3},{3,4},{4,5},{5,6},{6,7},{8,9},{9,10},{10,11},{11... | collective-permute-start | bytes 24584 | tf_op jit(solution)/shard_map/ppermute | solution.py:30
  331.4 5.0 %collective-permute-start.9 = (bf16[16,256]{1,0:T(8,128)(2,1)S(1)}, bf16[16,256]{1,0:T(8,128)(2,1)S(1)}, u32[]{:S(2)}, u32[]{:S(2)}) collective-permute-start(bf16[16,256]{1,0:T(8,128)(2,1)S(1)} %get-tuple-element.10), channel_id=1, source_target_pairs={{1,0},{2,1},{3,2},{4,3},{5,4},{6,5},{7,6},{9,8},{10,9},{11,10},{12... | collective-permute-start | bytes 24584 | tf_op jit(solution)/shard_map/ppermute | solution.py:33
  343.0 4.3 %collective-permute-start.10 = (bf16[16,256]{1,0:T(8,128)(2,1)S(1)}, bf16[16,256]{1,0:T(8,128)(2,1)S(1)}, u32[]{:S(2)}, u32[]{:S(2)}) collective-permute-start(bf16[16,256]{1,0:T(8,128)(2,1)S(1)} %get-tuple-element.7), channel_id=1, source_target_pairs={{0,1},{1,2},{2,3},{3,4},{4,5},{5,6},{6,7},{8,9},{9,10},{10,11},{11... | collective-permute-start | bytes 24584 | tf_op jit(solution)/shard_map/ppermute | solution.py:30
  345.0 5.0 %collective-permute-start.11 = (bf16[16,256]{1,0:T(8,128)(2,1)S(1)}, bf16[16,256]{1,0:T(8,128)(2,1)S(1)}, u32[]{:S(2)}, u32[]{:S(2)}) collective-permute-start(bf16[16,256]{1,0:T(8,128)(2,1)S(1)} %get-tuple-element.8), channel_id=1, source_target_pairs={{1,0},{2,1},{3,2},{4,3},{5,4},{6,5},{7,6},{9,8},{10,9},{11,10},{12... | collective-permute-start | bytes 24584 | tf_op jit(solution)/shard_map/ppermute | solution.py:33
  356.6 4.3 %collective-permute-start.12 = (bf16[16,256]{1,0:T(8,128)(2,1)S(1)}, bf16[16,256]{1,0:T(8,128)(2,1)S(1)}, u32[]{:S(2)}, u32[]{:S(2)}) collective-permute-start(bf16[16,256]{1,0:T(8,128)(2,1)S(1)} %get-tuple-element.5), channel_id=1, source_target_pairs={{0,1},{1,2},{2,3},{3,4},{4,5},{5,6},{6,7},{8,9},{9,10},{10,11},{11... | collective-permute-start | bytes 24584 | tf_op jit(solution)/shard_map/ppermute | solution.py:30
  358.6 5.0 %collective-permute-start.13 = (bf16[16,256]{1,0:T(8,128)(2,1)S(1)}, bf16[16,256]{1,0:T(8,128)(2,1)S(1)}, u32[]{:S(2)}, u32[]{:S(2)}) collective-permute-start(bf16[16,256]{1,0:T(8,128)(2,1)S(1)} %get-tuple-element.6), channel_id=1, source_target_pairs={{1,0},{2,1},{3,2},{4,3},{5,4},{6,5},{7,6},{9,8},{10,9},{11,10},{12... | collective-permute-start | bytes 24584 | tf_op jit(solution)/shard_map/ppermute | solution.py:33
